TPU v7x, 32 devices: a whole 2x2x4 slice. The times are simulated.
32 devices in a mesh: gx: 8 (over z, y), gy: 4 (over x, core).
Axes of the slice: x: 2, y: 2, z: 4, core: 2. Of those that a mesh axis runs over, the one named last changes fastest.
Arguments:
- psi: float32 [2, 256, 16, 1024], P(None, 'gx', None, 'gy'), may hold values from -6 to 6
- potential: float32 [256, 16, 1024], P('gx', None, 'gy'), may hold values from 0 to 4
Outputs:
- psi_half: float32 [2, 256, 16, 1024], P(None, 'gx', None, 'gy')
All inputs are finite; a program needn't handle non-finite values.
Results may differ from a plain program's by a relative error of at most 0.00005.
Values sent between devices are 32-bit elements; how exact they have to be, the bound alone decides.
A program may use at most 64 MiB of HBM per device.

v0:
```python
import jax
import jax.numpy as jnp
import numpy as np
from jax import lax
from jax.sharding import PartitionSpec as P

RYZ = 2


def with_halo(value, sides, width):
    for axis, dim in sides:
        peers, length = (lax.axis_size(axis), value.shape[dim])
        up = [(i, (i + 1) % peers) for i in range(peers - 1)]
        down = [(j, i) for i, j in up]
        last = lax.slice_in_dim(value, length - width, length, axis=dim)
        first = lax.slice_in_dim(value, 0, width, axis=dim)
        before = lax.ppermute(last, axis, up)
        after = lax.ppermute(first, axis, down)
        value = jnp.concatenate([before, value, after], axis=dim)
    return value


def cmul(left, right):
    return jnp.stack(
        [left[0] * right[0] - left[1] * right[1], left[0] * right[1] + left[1] * right[0]]
    )


def cinv(value):
    denom = value[0] * value[0] + value[1] * value[1]
    return jnp.stack([value[0] / denom, -value[1] / denom])


def local_inverse(cells):
    coef = 256.0 * cells * cells
    identity = np.eye(cells)
    cp_re_list = []
    cp_im_list = []
    dp_re_list = []
    dp_im_list = []
    cp_re = 0.0
    cp_im = 0.0
    dp_re = np.zeros(cells)
    dp_im = np.zeros(cells)
    for index in range(cells):
        piv_re = 1.0 - coef * cp_im
        piv_im = 2.0 * coef + coef * cp_re
        denom = piv_re * piv_re + piv_im * piv_im
        cp_re = -coef * piv_im / denom
        cp_im = -coef * piv_re / denom
        num_re = identity[index] - coef * dp_im
        num_im = coef * dp_re
        dp_re = (num_re * piv_re + num_im * piv_im) / denom
        dp_im = (num_im * piv_re - num_re * piv_im) / denom
        cp_re_list.append(cp_re)
        cp_im_list.append(cp_im)
        dp_re_list.append(dp_re)
        dp_im_list.append(dp_im)
    inv_re = np.zeros((cells, cells))
    inv_im = np.zeros((cells, cells))
    later_re = np.zeros(cells)
    later_im = np.zeros(cells)
    for index in range(cells - 1, -1, -1):
        next_re = dp_re_list[index] - (cp_re_list[index] * later_re - cp_im_list[index] * later_im)
        next_im = dp_im_list[index] - (cp_re_list[index] * later_im + cp_im_list[index] * later_re)
        later_re, later_im = (next_re, next_im)
        inv_re[index] = later_re
        inv_im[index] = later_im
    return (inv_re, inv_im, coef)


def shards(psi, potential):
    cells = psi.shape[1]
    count = lax.axis_size("gx")
    place = lax.axis_index("gx")
    inv_re, inv_im, coef = local_inverse(cells)
    upper_half = np.concatenate([inv_re, -inv_im], axis=1)
    lower_half = np.concatenate([inv_im, inv_re], axis=1)
    big = np.concatenate([upper_half, lower_half], axis=0).astype(np.float32)
    g_vec = jnp.asarray(np.stack([-coef * inv_im[:, 0], coef * inv_re[:, 0]]).astype(np.float32))
    h_vec = jnp.asarray(
        np.stack([-coef * inv_im[:, cells - 1], coef * inv_re[:, cells - 1]]).astype(np.float32)
    )
    s_val = g_vec[:, 0]
    t_val = g_vec[:, cells - 1]
    real_part, imag_part = (psi[0], psi[1])
    theta = 0.5 * (potential + real_part * real_part + imag_part * imag_part)
    cosine, sine = (jnp.cos(theta), jnp.sin(theta))
    turned = jnp.stack(
        [real_part * cosine + imag_part * sine, imag_part * cosine - real_part * sine]
    )
    padded = with_halo(turned, (("gy", 3),), 1)
    lap_y = padded[:, :, :, 2:] + padded[:, :, :, :-2] - 2.0 * turned
    z_padded = jnp.pad(turned, ((0, 0), (0, 0), (1, 1), (0, 0)))
    lap_z = z_padded[:, :, 2:] + z_padded[:, :, :-2] - 2.0 * turned
    side = RYZ * (lap_y + lap_z)
    rhs = jnp.stack([2.0 * turned[0] - side[1], 2.0 * turned[1] + side[0]])
    planes = rhs.shape[2]
    lines = rhs.shape[3]
    flat = rhs.reshape(2 * cells, planes * lines)
    local = jnp.dot(jnp.asarray(big), flat, precision=lax.Precision.HIGHEST).reshape(
        2, cells, planes, lines
    )
    first_val = local[:, 0]
    last_val = local[:, cells - 1]

    def advance(alpha, unused):
        q_val = cinv(
            jnp.stack(
                [
                    1.0 - (s_val[0] * alpha[0] - s_val[1] * alpha[1]),
                    -(s_val[0] * alpha[1] + s_val[1] * alpha[0]),
                ]
            )
        )
        aq_val = cmul(alpha, q_val)
        c_val = cmul(t_val, jnp.stack([1.0, 0.0]) + cmul(aq_val, s_val))
        mu_val = cmul(q_val, t_val)
        new_alpha = s_val + cmul(cmul(t_val, t_val), aq_val)
        return (new_alpha, (alpha, q_val, c_val, mu_val))

    unused, tables = lax.scan(advance, jnp.zeros((2,), jnp.float32), None, length=count)
    alphas, q_vals, c_vals, mu_vals = tables
    alpha_here = lax.dynamic_index_in_dim(alphas, place, 0, keepdims=False)
    q_here = lax.dynamic_index_in_dim(q_vals, place, 0, keepdims=False)
    mu_here = lax.dynamic_index_in_dim(mu_vals, place, 0, keepdims=False)
    fwd_term = last_val + cmul(cmul(t_val, cmul(alpha_here, q_here)), first_val)
    positions = jnp.arange(count, dtype=jnp.int32)

    def fwd_row(row, item):
        factor, index = item
        onehot = jnp.stack(
            [(positions == index).astype(jnp.float32), jnp.zeros((count,), jnp.float32)]
        )
        return (cmul(factor, row) + onehot, row)

    unused, fwd_rows = lax.scan(fwd_row, jnp.zeros((2, count), jnp.float32), (c_vals, positions))
    fwd_weights = lax.dynamic_index_in_dim(fwd_rows, place, 0, keepdims=False)
    piece = lax.all_gather(fwd_term[None], "gx", axis=0, tiled=True)
    weights = lax.slice_in_dim(fwd_weights, 0, piece.shape[0], axis=1)
    part_re = jnp.einsum(
        "k,kzy->zy", weights[0], piece[:, 0], precision=lax.Precision.HIGHEST
    ) - jnp.einsum("k,kzy->zy", weights[1], piece[:, 1], precision=lax.Precision.HIGHEST)
    part_im = jnp.einsum(
        "k,kzy->zy", weights[0], piece[:, 1], precision=lax.Precision.HIGHEST
    ) + jnp.einsum("k,kzy->zy", weights[1], piece[:, 0], precision=lax.Precision.HIGHEST)
    beta_prev = jnp.zeros_like(fwd_term) + jnp.stack([part_re, part_im])
    nu_here = cmul(q_here, first_val + cmul(s_val, beta_prev))

    def back_row(row, item):
        factor, index = item
        onehot = jnp.stack(
            [(positions == index).astype(jnp.float32), jnp.zeros((count,), jnp.float32)]
        )
        return (cmul(factor, row) + onehot, row)

    unused, back_rows = lax.scan(
        back_row, jnp.zeros((2, count), jnp.float32), (mu_vals, positions), reverse=True
    )
    back_weights = lax.dynamic_index_in_dim(back_rows, place, 0, keepdims=False)
    piece = lax.all_gather(nu_here[None], "gx", axis=0, tiled=True)
    weights = lax.slice_in_dim(back_weights, 0, piece.shape[0], axis=1)
    part_re = jnp.einsum(
        "k,kzy->zy", weights[0], piece[:, 0], precision=lax.Precision.HIGHEST
    ) - jnp.einsum("k,kzy->zy", weights[1], piece[:, 1], precision=lax.Precision.HIGHEST)
    part_im = jnp.einsum(
        "k,kzy->zy", weights[0], piece[:, 1], precision=lax.Precision.HIGHEST
    ) + jnp.einsum("k,kzy->zy", weights[1], piece[:, 0], precision=lax.Precision.HIGHEST)
    next_first = jnp.zeros_like(nu_here) + jnp.stack([part_re, part_im])
    first_here = cmul(mu_here, next_first) + nu_here
    edge_prev = cmul(alpha_here, first_here) + beta_prev
    from_left = cmul(g_vec[:, :, None, None], edge_prev[:, None])
    from_right = cmul(h_vec[:, :, None, None], next_first[:, None])
    return local + from_left + from_right - turned


def solution(mesh):
    return jax.shard_map(
        shards,
        mesh=mesh,
        in_specs=(P(None, "gx", None, "gy"), P("gx", None, "gy")),
        out_specs=P(None, "gx", None, "gy"),
        check_vma=False,
    )
```

profile of v0, /device:TPU:0, one launch (start us, length us, event | category | flops | bytes accessed | tf_op | source)
XLA Modules:
  0.0 309.6 jit_solution(17856614827695865240)
XLA Ops:
  0.0 3.6 %fusion.18 = (f32[32,16,256]{2,1,0:T(8,128)S(1)}, f32[32,16,256]{2,1,0:T(8,128)S(1)}) fusion(f32[2,32,16,256]{3,2,1,0:T(8,128)} %param.11, f32[32,16,256]{2,1,0:T(8,128)} %param.12), kind=kLoop, calls=%fused_computation.56 | loop fusion | flops 1441792 | bytes 2621440 | tf_op jit(solution)/shard_map/add | solution.py:90
  3.9 1.3 collective-permute-start
  5.2 3.8 %collective-permute-start.1 = (f32[2,32,16,1]{3,2,1,0:T(8,128)S(1)}, f32[2,32,16,1]{3,2,1,0:T(8,128)}, u32[]{:S(2)}, u32[]{:S(2)}) collective-permute-start(f32[2,32,16,1]{3,2,1,0:T(8,128)S(1)} %get-tuple-element.456), channel_id=1, source_target_pairs={{0,1},{1,2},{2,3},{4,5},{5,6},{6,7},{8,9},{9,10},{10,11},{12,13},{... | collective-permute-start | bytes 12296 | tf_op jit(solution)/shard_map/ppermute | solution.py:17
  9.7 162.3 %while.56 = (s32[]{:T(128)}, f32[2]{0:T(128)S(1)}, f32[8,2]{1,0:T(8,128)S(1)}, f32[8,2]{1,0:T(8,128)S(1)}, f32[8,2]{1,0:T(8,128)S(1)}, /*index=5*/f32[8,2]{1,0:T...) while((s32[]{:T(128)}, f32[2]{0:T(128)S(1)}, ...), condition=%wide.region_1.2_spmd.clone.clone, body=%wide.region_0.1_spmd.clone.clone.sunk | while | flops 63 | bytes 928 | solution.py:122
  173.8 26.4 %while.55 = (s32[]{:T(128)}, f32[2,8]{1,0:T(2,128)S(1)}, f32[8,2,8]{2,1,0:T(2,128)S(1)}, f32[8,2]{1,0:T(8,128)S(1)}, s32[8]{0:T(128)S(1)}, /*index=5*/s32[]{:T(128)}, s32[]{:T(128)}) while((s32[]{:T(128)}, f32[2,8]{1,0:T(2,128)S(1)}, f32[8,2,8]{2,1,0:T(2,128)S(1)}, f32[8,2]{1,0:T(8,128)S(1)}, s32[8]{0:T(128)S(1)}, ...), condition=%wide.region_5.6_spmd.clone.clone, body=%wide.region_4.5_spmd.clone.clone.sunk | while | flops 123 | bytes 3535 | solution.py:137
  175.8 1.3 multiply_subtract_fusion.10
  177.8 0.7 compare_bitcast_fusion.5
  179.1 1.3 multiply_subtract_fusion.10
  182.4 1.3 multiply_subtract_fusion.10
  185.7 1.3 multiply_subtract_fusion.10
  189.0 1.3 multiply_subtract_fusion.10
  192.3 1.3 multiply_subtract_fusion.10
  195.7 1.3 multiply_subtract_fusion.10
  199.0 1.3 multiply_subtract_fusion.10
  200.3 26.6 %while.54 = (s32[]{:T(128)}, f32[2,8]{1,0:T(2,128)S(1)}, f32[8,2,8]{2,1,0:T(2,128)S(1)}, f32[8,2]{1,0:T(8,128)S(1)}, s32[8]{0:T(128)S(1)}, /*index=5*/s32[]{:T(128)}, s32[]{:T(128)}, s32[]{:T(128)}) while((s32[]{:T(128)}, f32[2,8]{1,0:T(2,128)S(1)}, f32[8,2,8]{2,1,0:T(2,128)S(1)}, f32[8,2]{1,0:T(8,128)S(1)}, ...), condition=%wide.region_3.4_spmd.clone.clone, body=%wide.region_2.3_spmd.clone.clone.sunk | while | flops 124 | bytes 3555 | solution.py:157
  202.3 1.3 multiply_subtract_fusion.9
  205.6 1.3 multiply_subtract_fusion.9
  208.9 1.3 multiply_subtract_fusion.9
  212.2 1.3 multiply_subtract_fusion.9
  215.6 1.3 multiply_subtract_fusion.9
  218.9 1.3 multiply_subtract_fusion.9
  222.2 1.3 multiply_subtract_fusion.9
  225.5 1.3 multiply_subtract_fusion.9
  232.1 1.9 fusion.5
  235.1 1.0 fusion.68
  236.5 32.7 %all_gather.6 = f32[8,2,16,256]{3,2,1,0:T(8,128)S(1)} all-gather(f32[1,2,16,256]{3,2,1,0:T(8,128)S(1)} %fusion.37), channel_id=1, replica_groups=mesh['gx'=8,'gy'=4] {'gx'}, dimensions={0}, use_global_device_ids=true | all-gather | bytes 294912 | tf_op jit(solution)/shard_map/all_gather | solution.py:139
  270.6 1.3 multiply_subtract_fusion.5
  271.9 30.7 %all-gather = f32[16,16,256]{2,1,0:T(8,128)S(1)} all-gather(f32[2,16,256]{2,1,0:T(8,128)S(1)} %pad_maximum_fusion.6), channel_id=2, replica_groups=mesh['gx'=8,'gy'=4] {'gx'}, dimensions={0}, use_global_device_ids=true | all-gather | bytes 294912 | tf_op jit(solution)/shard_map/all_gather | solution.py:161
  303.9 1.2 subtract_bitcast_fusion
  305.1 1.2 add_bitcast_fusion
  306.4 1.4 multiply_subtract_fusion.4
  308.2 1.5 fusion.9
  (269 shorter events, 56.4 us)
Async XLA Ops:
  3.9 228.2 %collective-permute-start = (f32[2,32,16,1]{3,2,1,0:T(8,128)S(1)}, f32[2,32,16,1]{3,2,1,0:T(8,128)}, u32[]{:S(2)}, u32[]{:S(2)}) collective-permute-start(f32[2,32,16,1]{3,2,1,0:T(8,128)S(1)} %get-tuple-element.455), channel_id=1, source_target_pairs={{1,0},{2,1},{3,2},{5,4},{6,5},{7,6},{9,8},{10,9},{11,10},{13,12},{... | collective-permute-start | bytes 12296 | tf_op jit(solution)/shard_map/ppermute | solution.py:18
  5.2 226.9 %collective-permute-start.1 = (f32[2,32,16,1]{3,2,1,0:T(8,128)S(1)}, f32[2,32,16,1]{3,2,1,0:T(8,128)}, u32[]{:S(2)}, u32[]{:S(2)}) collective-permute-start(f32[2,32,16,1]{3,2,1,0:T(8,128)S(1)} %get-tuple-element.456), channel_id=1, source_target_pairs={{0,1},{1,2},{2,3},{4,5},{5,6},{6,7},{8,9},{9,10},{10,11},{12,13},{... | collective-permute-start | bytes 12296 | tf_op jit(solution)/shard_map/ppermute | solution.py:17
  9.0 0.7 copy-start
  9.0 0.7 copy-start.1
  9.0 0.7 copy-start.3
  234.4 0.8 copy-start.2
  270.6 37.2 %copy-start.6 = (f32[32]{0:T(128)S(1)}, f32[32]{0:T(128)}, u32[]{:S(2)}) copy-start(f32[32]{0:T(128)} %constant.154) | copy-start | bytes 388
  270.6 37.2 %copy-start.7 = (f32[32]{0:T(128)S(1)}, f32[32]{0:T(128)}, u32[]{:S(2)}) copy-start(f32[32]{0:T(128)} %constant.152) | copy-start | bytes 388
  302.9 5.0 %copy-start.4 = (f32[32]{0:T(128)S(1)}, f32[32]{0:T(128)}, u32[]{:S(2)}) copy-start(f32[32]{0:T(128)} %constant.150) | copy-start | bytes 388
  303.0 5.0 %copy-start.5 = (f32[32]{0:T(128)S(1)}, f32[32]{0:T(128)}, u32[]{:S(2)}) copy-start(f32[32]{0:T(128)} %constant.131) | copy-start | bytes 388
where the time goes:
time: 313 us; the launch traced here: 310 us
  loops' own time  144 us (46%)
  blocking collectives  63.5 us (20%)
  other arithmetic  47.9 us (15%)
  local copies, waits for them, and re-layouts  39.6 us (13%)
  between operations  5.62 us (2%)
  starting transfers between devices  5.13 us (2%)
  matrix products  3.47 us (1%)
    another operation x1, loops' own time, shards(): lax.scan(advance, jnp.zeros((2,), jnp.float32), None, length=count)  144 us
    all_gather x1, blocking collectives, shards(): piece = lax.all_gather(fwd_term[None], 'gx', axis=0, tiled=True)  32.7 us
    all_gather x1, blocking collectives, shards(): piece = lax.all_gather(nu_here[None], 'gx', axis=0, tiled=True)  30.7 us
    sub x21, other arithmetic, cmul(): left[0] * right[0] - left[1] * right[1]  23.7 us
    slice x18, local copies, waits for them, and re-layouts, cmul(): left[0] * right[0] - left[1] * right[1]  11.3 us
    dynamic_slice x32, local copies, waits for them, and re-layouts, shards(): lax.scan(fwd_row, jnp.zeros((2, count), jnp.float32), (c_vals, positions))  10.4 us
  transfers between devices with their start and end apart: 2, of which 0 were waited for; matrix products, arithmetic and copies ran while one was open for 23% of the time, Pallas kernels for 0%

commit v1 on v0

--- a/solution.py
+++ b/solution.py
@@ -136,7 +136,12 @@
 
     unused, fwd_rows = lax.scan(fwd_row, jnp.zeros((2, count), jnp.float32), (c_vals, positions))
     fwd_weights = lax.dynamic_index_in_dim(fwd_rows, place, 0, keepdims=False)
-    piece = lax.all_gather(fwd_term[None], "gx", axis=0, tiled=True)
+    ring = [fwd_term[None]]
+    for hop in range(7):
+        ring.append(lax.ppermute(ring[-1], "gx", [(dev, (dev + 1) % 8) for dev in range(8)]))
+    piece = jnp.roll(
+        jnp.concatenate(ring[::-1], axis=0), (lax.axis_index("gx") + 1) * ring[0].shape[0], axis=0
+    )
     weights = lax.slice_in_dim(fwd_weights, 0, piece.shape[0], axis=1)
     part_re = jnp.einsum(
         "k,kzy->zy", weights[0], piece[:, 0], precision=lax.Precision.HIGHEST

time: 313 us -> 303 us (0.968)
  blocking collectives: 63.5 us -> 30.7 us
  waiting for transfers between devices: 0.01 us -> 30.8 us
  loops' own time: 144 us -> 138 us
  other arithmetic: 47.9 us -> 44.1 us
  starting transfers between devices: 5.13 us -> 8.32 us
    all_gather x1 -> x0, blocking collectives: 32.7 us -> none  [shards(): piece = lax.all_gather(fwd_term[None], 'gx', axis=0, tiled=True)]
    ppermute x0 -> x7, waiting for transfers between devices: none -> 30.8 us  [shards(): lax.ppermute(ring[-1], 'gx', [(dev, (dev + 1) % 8) for dev in range(8)])]
    another operation x1, loops' own time: 144 us -> 137 us  [shards(): lax.scan(advance, jnp.zeros((2,), jnp.float32), None, length=count)]
    ppermute x0 -> x7, starting transfers between devices: none -> 3.18 us  [shards(): lax.ppermute(ring[-1], 'gx', [(dev, (dev + 1) % 8) for dev in range(8)])]
  transfers between devices with their start and end apart: 2 -> 9, of which waited for: 0 -> 5; matrix products, arithmetic and copies ran while one was open for 23% -> 23% of each run, Pallas kernels for 0% -> 0%
where the time goes in v1:
time: 303 us; the launch traced here: 300 us
  loops' own time  138 us (46%)
  other arithmetic  44.1 us (15%)
  local copies, waits for them, and re-layouts  38.8 us (13%)
  waiting for transfers between devices  30.8 us (10%)
  blocking collectives  30.7 us (10%)
  starting transfers between devices  8.32 us (3%)
  between operations  5.62 us (2%)
  matrix products  3.46 us (1%)
    another operation x1, loops' own time, shards(): lax.scan(advance, jnp.zeros((2,), jnp.float32), None, length=count)  137 us
    ppermute x7, waiting for transfers between devices, shards(): lax.ppermute(ring[-1], 'gx', [(dev, (dev + 1) % 8) for dev in range(8)])  30.8 us
    all_gather x1, blocking collectives, shards(): piece = lax.all_gather(nu_here[None], 'gx', axis=0, tiled=True)  30.7 us
    sub x21, other arithmetic, cmul(): left[0] * right[0] - left[1] * right[1]  21.8 us
    slice x18, local copies, waits for them, and re-layouts, cmul(): left[0] * right[0] - left[1] * right[1]  11.6 us
    dynamic_slice x32, local copies, waits for them, and re-layouts, shards(): lax.scan(fwd_row, jnp.zeros((2, count), jnp.float32), (c_vals, positions))  9.06 us
  transfers between devices with their start and end apart: 9, of which 5 were waited for; matrix products, arithmetic and copies ran while one was open for 23% of the time, Pallas kernels for 0%

profile of v1, /device:TPU:0, one launch (start us, length us, event | category | flops | bytes accessed | tf_op | source)
XLA Modules:
  0.0 300.0 jit_solution(10008975815166851012)
XLA Ops:
  0.0 3.6 %fusion.18 = (f32[32,16,256]{2,1,0:T(8,128)S(1)}, f32[32,16,256]{2,1,0:T(8,128)S(1)}) fusion(f32[2,32,16,256]{3,2,1,0:T(8,128)} %param.11, f32[32,16,256]{2,1,0:T(8,128)} %param.12), kind=kLoop, calls=%fused_computation.56 | loop fusion | flops 1441792 | bytes 2621440 | tf_op jit(solution)/shard_map/add | solution.py:90
  3.9 1.3 collective-permute-start
  5.2 3.8 %collective-permute-start.1 = (f32[2,32,16,1]{3,2,1,0:T(8,128)S(1)}, f32[2,32,16,1]{3,2,1,0:T(8,128)}, u32[]{:S(2)}, u32[]{:S(2)}) collective-permute-start(f32[2,32,16,1]{3,2,1,0:T(8,128)S(1)} %get-tuple-element.456), channel_id=1, source_target_pairs={{0,1},{1,2},{2,3},{4,5},{5,6},{6,7},{8,9},{9,10},{10,11},{12,13},{... | collective-permute-start | bytes 12296 | tf_op jit(solution)/shard_map/ppermute | solution.py:17
  9.7 156.3 %while.56 = (s32[]{:T(128)}, f32[2]{0:T(128)S(1)}, f32[8,2]{1,0:T(8,128)S(1)}, f32[8,2]{1,0:T(8,128)S(1)}, f32[8,2]{1,0:T(8,128)S(1)}, /*index=5*/f32[8,2]{1,0:T...) while((s32[]{:T(128)}, f32[2]{0:T(128)S(1)}, ...), condition=%wide.region_1.2_spmd.clone.clone, body=%wide.region_0.1_spmd.clone.clone.sunk | while | flops 63 | bytes 928 | solution.py:122
  172.3 1.9 fusion.5
  176.7 3.1 %collective-permute-start.2 = (f32[1,2,16,256]{3,2,1,0:T(8,128)S(1)}, f32[1,2,16,256]{3,2,1,0:T(8,128)S(1)}, u32[]{:S(2)}, u32[]{:S(2)}) collective-permute-start(f32[1,2,16,256]{3,2,1,0:T(8,128)S(1)} %fusion.37), channel_id=1, source_target_pairs={{0,4},{4,8},{8,12},{12,16},{16,20},{20,24},{24,28},{28,0},{1,5},{5... | collective-permute-start | bytes 98312 | tf_op jit(solution)/shard_map/ppermute | solution.py:141
  179.8 4.9 %collective-permute-done.2 = f32[1,2,16,256]{3,2,1,0:T(8,128)S(1)} collective-permute-done((f32[1,2,16,256]{3,2,1,0:T(8,128)S(1)}, f32[1,2,16,256]{3,2,1,0:T(8,128)S(1)}, u32[]{:S(2)}, u32[]{:S(2)}) %collective-permute-start.2) | collective-permute-done | bytes 32800 | tf_op jit(solution)/shard_map/ppermute | solution.py:141
  184.7 6.6 %collective-permute-done.3 = f32[1,2,16,256]{3,2,1,0:T(8,128)S(1)} collective-permute-done((f32[1,2,16,256]{3,2,1,0:T(8,128)S(1)}, f32[1,2,16,256]{3,2,1,0:T(8,128)S(1)}, u32[]{:S(2)}, u32[]{:S(2)}) %collective-permute-start.3) | collective-permute-done | bytes 32800 | tf_op jit(solution)/shard_map/ppermute | solution.py:141
  191.4 6.6 %collective-permute-done.4 = f32[1,2,16,256]{3,2,1,0:T(8,128)S(1)} collective-permute-done((f32[1,2,16,256]{3,2,1,0:T(8,128)S(1)}, f32[1,2,16,256]{3,2,1,0:T(8,128)S(1)}, u32[]{:S(2)}, u32[]{:S(2)}) %collective-permute-start.4) | collective-permute-done | bytes 32800 | tf_op jit(solution)/shard_map/ppermute | solution.py:141
  198.0 24.1 %while.54 = (s32[]{:T(128)}, f32[2,8]{1,0:T(2,128)S(1)}, f32[8,2,8]{2,1,0:T(2,128)S(1)}, f32[8,2]{1,0:T(8,128)S(1)}, s32[8]{0:T(128)S(1)}, /*index=5*/s32[]{:T(128)}, s32[]{:T(128)}, s32[]{:T(128)}) while((s32[]{:T(128)}, f32[2,8]{1,0:T(2,128)S(1)}, f32[8,2,8]{2,1,0:T(2,128)S(1)}, f32[8,2]{1,0:T(8,128)S(1)}, ...), condition=%wide.region_3.4_spmd.clone.clone, body=%wide.region_2.3_spmd.clone.clone.sunk | while | flops 124 | bytes 3555 | solution.py:162
  199.8 1.2 multiply_subtract_fusion.9
  202.8 1.2 multiply_subtract_fusion.9
  205.8 1.2 multiply_subtract_fusion.9
  208.8 1.2 multiply_subtract_fusion.9
  211.8 1.2 multiply_subtract_fusion.9
  214.8 1.2 multiply_subtract_fusion.9
  217.8 1.2 multiply_subtract_fusion.9
  220.8 1.2 multiply_subtract_fusion.9
  222.2 24.1 %while.55 = (s32[]{:T(128)}, f32[2,8]{1,0:T(2,128)S(1)}, f32[8,2,8]{2,1,0:T(2,128)S(1)}, f32[8,2]{1,0:T(8,128)S(1)}, s32[8]{0:T(128)S(1)}, /*index=5*/s32[]{:T(128)}, s32[]{:T(128)}) while((s32[]{:T(128)}, f32[2,8]{1,0:T(2,128)S(1)}, f32[8,2,8]{2,1,0:T(2,128)S(1)}, f32[8,2]{1,0:T(8,128)S(1)}, s32[8]{0:T(128)S(1)}, ...), condition=%wide.region_5.6_spmd.clone.clone, body=%wide.region_4.5_spmd.clone.clone.sunk | while | flops 123 | bytes 3535 | solution.py:137
  224.0 1.2 multiply_subtract_fusion.10
  227.0 1.2 multiply_subtract_fusion.10
  230.0 1.2 multiply_subtract_fusion.10
  233.0 1.2 multiply_subtract_fusion.10
  236.0 1.2 multiply_subtract_fusion.10
  239.0 1.2 multiply_subtract_fusion.10
  246.9 6.0 %collective-permute-done.7 = f32[1,2,16,256]{3,2,1,0:T(8,128)S(1)} collective-permute-done((f32[1,2,16,256]{3,2,1,0:T(8,128)S(1)}, f32[1,2,16,256]{3,2,1,0:T(8,128)S(1)}, u32[]{:S(2)}, u32[]{:S(2)}) %collective-permute-start.7) | collective-permute-done | bytes 32800 | tf_op jit(solution)/shard_map/ppermute | solution.py:141
  252.9 6.6 %collective-permute-done.8 = f32[1,2,16,256]{3,2,1,0:T(8,128)S(1)} collective-permute-done((f32[1,2,16,256]{3,2,1,0:T(8,128)S(1)}, f32[1,2,16,256]{3,2,1,0:T(8,128)S(1)}, u32[]{:S(2)}, u32[]{:S(2)}) %collective-permute-start.8) | collective-permute-done | bytes 32800 | tf_op jit(solution)/shard_map/ppermute | solution.py:141
  261.1 1.4 multiply_subtract_fusion.5
  262.5 30.7 %all-gather = f32[16,16,256]{2,1,0:T(8,128)S(1)} all-gather(f32[2,16,256]{2,1,0:T(8,128)S(1)} %pad_maximum_fusion.6), channel_id=2, replica_groups=mesh['gx'=8,'gy'=4] {'gx'}, dimensions={0}, use_global_device_ids=true | all-gather | bytes 294912 | tf_op jit(solution)/shard_map/all_gather | solution.py:166
  294.5 1.2 subtract_bitcast_fusion
  295.7 1.2 add_bitcast_fusion
  298.6 1.5 fusion.9
  (297 shorter events, 59.2 us)
Async XLA Ops:
  3.9 168.5 %collective-permute-start = (f32[2,32,16,1]{3,2,1,0:T(8,128)S(1)}, f32[2,32,16,1]{3,2,1,0:T(8,128)}, u32[]{:S(2)}, u32[]{:S(2)}) collective-permute-start(f32[2,32,16,1]{3,2,1,0:T(8,128)S(1)} %get-tuple-element.455), channel_id=1, source_target_pairs={{1,0},{2,1},{3,2},{5,4},{6,5},{7,6},{9,8},{10,9},{11,10},{13,12},{... | collective-permute-start | bytes 12296 | tf_op jit(solution)/shard_map/ppermute | solution.py:18
  5.2 167.2 %collective-permute-start.1 = (f32[2,32,16,1]{3,2,1,0:T(8,128)S(1)}, f32[2,32,16,1]{3,2,1,0:T(8,128)}, u32[]{:S(2)}, u32[]{:S(2)}) collective-permute-start(f32[2,32,16,1]{3,2,1,0:T(8,128)S(1)} %get-tuple-element.456), channel_id=1, source_target_pairs={{0,1},{1,2},{2,3},{4,5},{5,6},{6,7},{8,9},{9,10},{10,11},{12,13},{... | collective-permute-start | bytes 12296 | tf_op jit(solution)/shard_map/ppermute | solution.py:17
  9.0 0.7 copy-start
  9.0 0.7 copy-start.1
  9.0 0.7 copy-start.3
  174.6 0.8 copy-start.2
  176.7 8.0 %collective-permute-start.2 = (f32[1,2,16,256]{3,2,1,0:T(8,128)S(1)}, f32[1,2,16,256]{3,2,1,0:T(8,128)S(1)}, u32[]{:S(2)}, u32[]{:S(2)}) collective-permute-start(f32[1,2,16,256]{3,2,1,0:T(8,128)S(1)} %fusion.37), channel_id=1, source_target_pairs={{0,4},{4,8},{8,12},{12,16},{16,20},{20,24},{24,28},{28,0},{1,5},{5... | collective-permute-start | bytes 98312 | tf_op jit(solution)/shard_map/ppermute | solution.py:141
  184.7 6.6 %collective-permute-start.3 = (f32[1,2,16,256]{3,2,1,0:T(8,128)S(1)}, f32[1,2,16,256]{3,2,1,0:T(8,128)S(1)}, u32[]{:S(2)}, u32[]{:S(2)}) collective-permute-start(f32[1,2,16,256]{3,2,1,0:T(8,128)S(1)} %collective-permute-done.2), channel_id=1, source_target_pairs={{0,4},{4,8},{8,12},{12,16},{16,20},{20,24},{24,28},{28,0},{1,5},{5... | collective-permute-start | bytes 98312 | tf_op jit(solution)/shard_map/ppermute | solution.py:141
  191.3 6.6 %collective-permute-start.4 = (f32[1,2,16,256]{3,2,1,0:T(8,128)S(1)}, f32[1,2,16,256]{3,2,1,0:T(8,128)S(1)}, u32[]{:S(2)}, u32[]{:S(2)}) collective-permute-start(f32[1,2,16,256]{3,2,1,0:T(8,128)S(1)} %collective-permute-done.3), channel_id=1, source_target_pairs={{0,4},{4,8},{8,12},{12,16},{16,20},{20,24},{24,28},{28,0},{1,5},{5... | collective-permute-start | bytes 98312 | tf_op jit(solution)/shard_map/ppermute | solution.py:141
  198.0 24.1 %collective-permute-start.5 = (f32[1,2,16,256]{3,2,1,0:T(8,128)S(1)}, f32[1,2,16,256]{3,2,1,0:T(8,128)S(1)}, u32[]{:S(2)}, u32[]{:S(2)}) collective-permute-start(f32[1,2,16,256]{3,2,1,0:T(8,128)S(1)} %collective-permute-done.4), channel_id=1, source_target_pairs={{0,4},{4,8},{8,12},{12,16},{16,20},{20,24},{24,28},{28,0},{1,5},{5... | collective-permute-start | bytes 98312 | tf_op jit(solution)/shard_map/ppermute | solution.py:141
  222.1 24.2 %collective-permute-start.6 = (f32[1,2,16,256]{3,2,1,0:T(8,128)S(1)}, f32[1,2,16,256]{3,2,1,0:T(8,128)S(1)}, u32[]{:S(2)}, u32[]{:S(2)}) collective-permute-start(f32[1,2,16,256]{3,2,1,0:T(8,128)S(1)} %collective-permute-done.5), channel_id=1, source_target_pairs={{0,4},{4,8},{8,12},{12,16},{16,20},{20,24},{24,28},{28,0},{1,5},{5... | collective-permute-start | bytes 98312 | tf_op jit(solution)/shard_map/ppermute | solution.py:141
  246.2 6.7 %collective-permute-start.7 = (f32[1,2,16,256]{3,2,1,0:T(8,128)S(1)}, f32[1,2,16,256]{3,2,1,0:T(8,128)S(1)}, u32[]{:S(2)}, u32[]{:S(2)}) collective-permute-start(f32[1,2,16,256]{3,2,1,0:T(8,128)S(1)} %collective-permute-done.6), channel_id=1, source_target_pairs={{0,4},{4,8},{8,12},{12,16},{16,20},{20,24},{24,28},{28,0},{1,5},{5... | collective-permute-start | bytes 98312 | tf_op jit(solution)/shard_map/ppermute | solution.py:141
  252.9 6.6 %collective-permute-start.8 = (f32[1,2,16,256]{3,2,1,0:T(8,128)S(1)}, f32[1,2,16,256]{3,2,1,0:T(8,128)S(1)}, u32[]{:S(2)}, u32[]{:S(2)}) collective-permute-start(f32[1,2,16,256]{3,2,1,0:T(8,128)S(1)} %collective-permute-done.7), channel_id=1, source_target_pairs={{0,4},{4,8},{8,12},{12,16},{16,20},{20,24},{24,28},{28,0},{1,5},{5... | collective-permute-start | bytes 98312 | tf_op jit(solution)/shard_map/ppermute | solution.py:141
  261.0 37.1 %copy-start.6 = (f32[32]{0:T(128)S(1)}, f32[32]{0:T(128)}, u32[]{:S(2)}) copy-start(f32[32]{0:T(128)} %constant.176) | copy-start | bytes 388
  261.1 37.1 %copy-start.7 = (f32[32]{0:T(128)S(1)}, f32[32]{0:T(128)}, u32[]{:S(2)}) copy-start(f32[32]{0:T(128)} %constant.174) | copy-start | bytes 388
  293.6 4.8 %copy-start.4 = (f32[32]{0:T(128)S(1)}, f32[32]{0:T(128)}, u32[]{:S(2)}) copy-start(f32[32]{0:T(128)} %constant.172) | copy-start | bytes 388
  293.6 4.8 %copy-start.5 = (f32[32]{0:T(128)S(1)}, f32[32]{0:T(128)}, u32[]{:S(2)}) copy-start(f32[32]{0:T(128)} %constant.153) | copy-start | bytes 388
